TPU v7x, 32 devices: a whole 2x2x4 slice. The times are simulated.
32 devices in a mesh: groups: 2 (over y), tm: 16 (over z, x, core).
Axes of the slice: x: 2, y: 2, z: 4, core: 2. Of those that a mesh axis runs over, the one named last changes fastest.
Arguments:
- voltages: bfloat16 [256, 256, 2, 188], P(None, ('groups', 'tm')), parts along dimension 1, as said below
- off_starts: int32 [16], P('groups'), parts along dimension 0, may hold values from 0 to 124, as said below
- pointing: int32 [36], replicated, may hold values from 0 to 2047, as said below
- patterns: bfloat16 [2, 188, 2048], P(None, None, 'tm'), may hold values from -0.3125 to 0.3125
Outputs:
- beam_weights: bfloat16 [512, 2, 6768], P(('groups', 'tm')), parts along dimension 0
- beam_maps: float32 [512, 36, 2048], P('groups', None, 'tm'), parts along dimension 0
There are 2 independent parts, one for each index of `groups`. A program takes and returns all parts, laid end to end along the dimension named above; an argument that names none is the same for every part. Nothing has to cross between parts.
Inputs may be any that keep to these rules, and one draw needn't show every extreme that they name: Complex port voltages: thermal noise whose power differs between ports and grows along time, plus sky signals common to the ports. `off_starts`: each of the 8 off-source ranges covers 4 samples from this start; ranges may intersect. `pointing`: several beams may point at the same pixel.
All inputs are finite; a program needn't handle non-finite values.
Results may differ from a plain program's by a relative error of at most 0.0034.
Values may be sent and summed in bfloat16 or wider, within the bound.
No kernel may reach another device: no remote copies, remote signals or barrier semaphores. Data moves between devices by JAX's collectives and lax.ppermute only.
A program may use at most 64 MiB of HBM per device.

v0:
```python
import jax
import jax.numpy as jnp
from jax import lax
from jax.sharding import PartitionSpec as P

ITERS = 20
highest = lax.Precision.HIGHEST


def off_flags(moments, starts, range_len):
    shape_now = moments.shape
    flat_moments = moments.reshape(-1)
    inside = (flat_moments[None, :] >= starts[:, None]) & (
        flat_moments[None, :] < starts[:, None] + range_len
    )
    return jnp.any(inside, axis=0).reshape(shape_now)


def split_gram(products, port_count):
    corr_real = products[..., :port_count, :port_count] + products[..., port_count:, port_count:]
    corr_imag = products[..., port_count:, :port_count] - products[..., :port_count, port_count:]
    return jnp.stack([corr_real, corr_imag], axis=-3)


def beam_power(weights, patterns):
    port_count = weights.shape[3]
    real_rows = jnp.concatenate([weights[:, 0], weights[:, 1]], axis=-1)
    imag_rows = jnp.concatenate([-weights[:, 1], weights[:, 0]], axis=-1)
    rows_all = jnp.stack([real_rows, imag_rows], axis=2).reshape(-1, 2 * port_count)
    response = jnp.dot(
        rows_all, patterns.reshape(2 * port_count, -1), preferred_element_type=jnp.float32
    )
    response = response.reshape(weights.shape[0], weights.shape[2], 2, -1)
    return response[:, :, 0] * response[:, :, 0] + response[:, :, 1] * response[:, :, 1]


def on_device(voltages, off_starts, pointing, patterns):
    devices = lax.axis_size("tm")
    position = lax.axis_index("tm")
    channels = voltages.shape[0]
    samples_dev = voltages.shape[1]
    ports = voltages.shape[3]
    beams = pointing.shape[0]
    per_dev = channels // devices
    double_width = 2 * ports
    total_time = samples_dev * devices
    off_span = max(4, total_time // 32)
    every_moment = jnp.arange(total_time, dtype=jnp.int32)
    off_count = jnp.sum(off_flags(every_moment, off_starts, off_span).astype(jnp.float32))
    pixels = patterns.shape[2]
    pixel_ids = position * pixels + jnp.arange(pixels, dtype=jnp.int32)
    selector = (pixel_ids[:, None] == pointing[None, :]).astype(jnp.bfloat16)
    steer_local = jnp.einsum("rpx,xb->rpb", patterns, selector, preferred_element_type=jnp.float32)
    steering = lax.psum(steer_local, "tm")
    blocks = voltages.reshape(devices, per_dev, samples_dev, double_width)
    arrived = lax.all_to_all(blocks, "tm", split_axis=0, concat_axis=0, tiled=True)
    moments = (
        jnp.arange(devices, dtype=jnp.int32)[:, None] * samples_dev
        + jnp.arange(samples_dev, dtype=jnp.int32)[None, :]
    )
    is_off = off_flags(moments, off_starts, off_span)
    on_source = jnp.where(is_off[:, None, :, None], jnp.zeros_like(arrived), arrived)
    products = jnp.einsum("nksi,nksj->kij", on_source, arrived, preferred_element_type=jnp.float32)
    corr_mine = split_gram(products, ports)
    squared = jnp.square(arrived.astype(jnp.float32))
    powers = jnp.sum(jnp.where(is_off[:, None, :, None], squared, jnp.float32(0.0)), axis=(0, 2))
    noise_total = powers[:, :ports] + powers[:, ports:]
    noise_power = noise_total / off_count + 1e-06
    scales = 1.0 / jnp.sqrt(noise_power)
    white_real = corr_mine[:, 0] * scales[:, :, None] * scales[:, None, :]
    white_imag = corr_mine[:, 1] * scales[:, :, None] * scales[:, None, :]
    steer_real = steering[0][None]
    steer_imag = steering[1][None]

    def apply_white(matrix, vector):
        return jnp.einsum("kij,kjb->kib", matrix, vector, precision=highest)

    def power_turn(counter, state_pair):
        beam_real, beam_imag = state_pair
        conj_real = steer_real * beam_real + steer_imag * beam_imag
        conj_imag = steer_real * beam_imag - steer_imag * beam_real
        mixed_real = apply_white(white_real, conj_real) - apply_white(white_imag, conj_imag)
        mixed_imag = apply_white(white_real, conj_imag) + apply_white(white_imag, conj_real)
        image_real = steer_real * mixed_real - steer_imag * mixed_imag
        image_imag = steer_real * mixed_imag + steer_imag * mixed_real
        mean_square = (
            jnp.sum(image_real * image_real, axis=1) + jnp.sum(image_imag * image_imag, axis=1)
        ) / (2 * ports)
        factor = 1.0 / jnp.sqrt(mean_square + 1e-06)
        return (image_real * factor[:, None, :], image_imag * factor[:, None, :])

    initial = (
        jnp.broadcast_to(steer_real, (per_dev, ports, beams)),
        jnp.broadcast_to(steer_imag, (per_dev, ports, beams)),
    )
    beam_real, beam_imag = lax.fori_loop(0, ITERS, power_turn, initial)
    weight_real = beam_real * scales[:, :, None]
    weight_imag = beam_imag * scales[:, :, None]
    weight_pair = (
        jnp.stack([weight_real, weight_imag], axis=1).transpose(0, 1, 3, 2).astype(jnp.bfloat16)
    )
    flat_pair = weight_pair.reshape(per_dev, 2, beams * ports)
    collected = lax.all_gather(flat_pair, "tm", axis=0, tiled=True)
    all_weights = collected.reshape(channels, 2, beams, ports)
    maps_out = beam_power(all_weights, patterns)
    return (flat_pair, maps_out)


def solution(mesh):
    in_specs = (P(None, ("groups", "tm"), None, None), P("groups"), P(), P(None, None, "tm"))
    out_specs = (P(("groups", "tm"), None, None), P("groups", None, "tm"))
    return jax.shard_map(
        on_device, mesh=mesh, in_specs=in_specs, out_specs=out_specs, check_vma=False
    )
```

profile of v0, /device:TPU:0, one launch (start us, length us, event | category | flops | bytes accessed | tf_op | source)
XLA Modules:
  0.0 552.6 jit_solution(12295495400840213857)
XLA Ops:
  7.2 7.9 %copy.28 = bf16[256,8,2,188]{3,2,1,0:T(2,128)(2,1)S(1)} copy(bf16[256,8,2,188]{0,2,3,1:T(2,128)(2,1)} %param.6) | data formatting | bytes 3080192 | tf_op args[0]
  17.1 7.4 %all-to-all-start = ((bf16[16,16,8,376]{3,2,1,0:T(8,128)(2,1)}), bf16[16,16,8,376]{3,2,1,0:T(8,128)(2,1)S(1)}, u32[]{:S(2)}, u32[]{:S(2)}) async-start(bf16[16,16,8,376]{3,2,1,0:T(8,128)(2,1)} %reshape.61), calls=%async_computation | async-start | bytes 3145728 | tf_op jit(solution)/shard_map/all_to_all | solution.py:56
  25.1 81.9 %psum.7 = f32[2,188,36]{1,2,0:T(8,128)S(1)} all-reduce(f32[2,188,36]{1,2,0:T(8,128)S(1)} %convolution_bitcast_fusion.1), channel_id=1, replica_groups=mesh['groups'=2,'tm'=16] {'tm'}, use_global_device_ids=true, to_apply=%region_0.0 | all-reduce | flops 13536 | bytes 108288 | tf_op jit(solution)/shard_map/psum | solution.py:54
  110.7 3.6 fusion.11
  116.0 321.7 %while.12 = (s32[]{:T(128)}, f32[16,188,36]{1,2,0:T(8,128)}, f32[16,188,36]{1,2,0:T(8,128)}, f32[1,188,36]{1,2,0:T(8,128)S(1)}, f32[1,188,36]{1,2,0:T(8,128)S(1)...) while((s32[]{:T(128)}, f32[16,188,36]{1,2,0:T(8,128)}, f32[16,188,36]{1,2,0:T(8,128)}, ...), condition=%wide.region_8.9_spmd, body=%wide.region_5.8_spmd.sunk | while | flops 980656704 | bytes 30075944 | solution.py:96
  116.0 5.4 fusion.50
  127.6 3.2 multiply_reduce_fusion.3
  132.1 5.4 fusion.50
  148.2 5.4 fusion.50
  164.3 5.4 fusion.50
  180.4 5.4 fusion.50
  196.4 5.4 fusion.50
  212.5 5.4 fusion.50
  228.6 5.4 fusion.50
  244.7 5.4 fusion.50
  260.8 5.4 fusion.50
  276.9 5.4 fusion.50
  292.9 5.4 fusion.50
  309.0 5.4 fusion.50
  325.1 5.4 fusion.50
  341.2 5.4 fusion.50
  357.3 5.4 fusion.50
  373.4 5.4 fusion.50
  389.5 5.4 fusion.50
  405.5 5.4 fusion.50
  421.6 5.4 fusion.50
  442.7 60.5 %all-gather.2.cloned.1.call-done = bf16[256,2,6768]{2,0,1:T(8,128)(2,1)} async-done(((bf16[16,2,6768]{2,0,1:T(8,128)(2,1)}), bf16[256,2,6768]{2,0,1:T(8,128)(2,1)}) %all-gather.2.cloned.1.call-update) | async-done | bytes 6930448 | tf_op jit(solution)/shard_map/all_gather | solution.py:103
  503.3 10.1 %copy.29 = bf16[256,2,6768]{0,2,1:T(8,128)(2,1)} copy(bf16[256,2,6768]{2,0,1:T(8,128)(2,1)} %all-gather.2.cloned.1.call-done) | data formatting | bytes 13860864 | tf_op jit(solution)/shard_map/all_gather | solution.py:103
  513.4 9.9 %reshape.63 = bf16[256,2,36,188]{0,3,2,1:T(8,128)(2,1)} reshape(bf16[256,2,6768]{0,2,1:T(8,128)(2,1)} %copy.29) | data formatting | bytes 13860864 | tf_op jit(solution)/shard_map/reshape | solution.py:104
  523.3 3.7 slice_bitcast_fusion
  528.6 7.0 %maximum_bitcast_fusion = (bf16[256,36,1,376]{0,3,2,1:T(8,128)(2,1)}, bf16[256,36,1,376]{0,3,2,1:T(8,128)(2,1)}) fusion(bf16[256,36,188]{0,2,1:T(8,128)(2,1)S(1)} %get-tuple-element.71, bf16[256,36,188]{0,2,1:T(8,128)(2,1)S(1)} %get-tuple-element.72, bf16[256,36,188]{0,2,1:T(8,128)(2,1)S(1)} %fusion.32), kind=kLoop, calls=%fused_computation.19 | loop fusion | flops 27721728 | bytes 24256512 | tf_op jit(solution)/shard_map/stack | solution.py:29
  535.6 7.2 %fusion.4 = f32[256,36,2,128]{3,0,2,1:T(8,128)S(1)} fusion(bf16[256,36,1,376]{0,3,2,1:T(8,128)(2,1)} %get-tuple-element.74, bf16[256,36,1,376]{0,3,2,1:T(8,128)(2,1)} %get-tuple-element.73, bf16[376,128,1,1]{1,0,2,3:T(8,128)(2,1)S(1)} %reshape.67), kind=kOutput, calls=%fused_computation.15 | convolution fusion | flops 1781121024 | bytes 23394304 | tf_op jit(solution)/shard_map/dot_general | solution.py:30
  (254 shorter events, 226.4 us)
Async XLA Ops:
  15.1 9.6 %copy-start.6 = (s32[8]{0:T(128)S(1)}, s32[8]{0:T(128)}, u32[]{:S(2)}) copy-start(s32[8]{0:T(128)} %param.7) | copy-start | bytes 100
  15.1 9.8 %copy-start.4 = (bf16[2,188,128]{2,0,1:T(2,128)(2,1)S(1)}, bf16[2,188,128]{2,0,1:T(2,128)(2,1)}, u32[]{:S(2)}) copy-start(bf16[2,188,128]{2,0,1:T(2,128)(2,1)} %param.9) | copy-start | bytes 288772
  15.1 9.8 %copy-start.5 = (s32[36]{0:T(128)S(1)}, s32[36]{0:T(128)}, u32[]{:S(2)}) copy-start(s32[36]{0:T(128)} %param.8) | copy-start | bytes 436
  17.1 90.5 %all-to-all-start = ((bf16[16,16,8,376]{3,2,1,0:T(8,128)(2,1)}), bf16[16,16,8,376]{3,2,1,0:T(8,128)(2,1)S(1)}, u32[]{:S(2)}, u32[]{:S(2)}) async-start(bf16[16,16,8,376]{3,2,1,0:T(8,128)(2,1)} %reshape.61), calls=%async_computation | async-start | bytes 3145728 | tf_op jit(solution)/shard_map/all_to_all | solution.py:56
  24.5 478.8 %all-gather.2.cloned.1.call-start = ((), (), s32[]{:S(2)}) async-start(), calls=%async_computation.1 | async-start | bytes 7380992 | tf_op jit(solution)/shard_map/all_gather | solution.py:103
  116.0 5.4 copy-start.2
  132.1 5.4 copy-start.1
  132.1 5.4 copy-start.2
  148.2 5.4 copy-start.1
  148.2 5.4 copy-start.2
  164.3 5.4 copy-start.1
  164.3 5.4 copy-start.2
  180.4 5.4 copy-start.1
  180.4 5.4 copy-start.2
  196.4 5.4 copy-start.1
  196.4 5.4 copy-start.2
  212.5 5.4 copy-start.1
  212.5 5.4 copy-start.2
  228.6 5.4 copy-start.2
  244.7 5.4 copy-start.2
  260.8 5.4 copy-start.2
  276.9 5.4 copy-start.2
  292.9 5.4 copy-start.2
  309.0 5.4 copy-start.2
  325.1 5.4 copy-start.2
  341.2 5.4 copy-start.2
  357.3 5.4 copy-start.2
  373.4 5.4 copy-start.2
  389.5 5.4 copy-start.2
  405.5 5.4 copy-start.2
  421.6 5.4 copy-start.1
  421.6 5.4 copy-start.2
  (34 other events, 137.7 us)
Sparse Core Ops, SparseCore 0:
  440.7 62.5 all-gather.1
where the time goes:
time: 553 us
  matrix products  303 us (55%)
  blocking collectives  81.9 us (15%)
  waiting for transfers between devices  60.6 us (11%)
  other arithmetic  43.2 us (8%)
  local copies, waits for them, and re-layouts  40.7 us (7%)
  between operations  14.2 us (3%)
  starting transfers between devices  7.43 us (1%)
    dot_general x80, matrix products, apply_white(): return jnp.einsum('kij,kjb->kib', matrix, vector, precision=highest)  294 us
    psum x1, blocking collectives, on_device(): steering = lax.psum(steer_local, 'tm')  81.9 us
    all_gather x1, waiting for transfers between devices, on_device(): collected = lax.all_gather(flat_pair, 'tm', axis=0, tiled=True)  60.5 us
    mul x20, other arithmetic, power_turn(): return (image_real * factor[:, None, :], image_imag * factor[:, None, :])  25.8 us
    unnamed x11, local copies, waits for them, and re-layouts  11.5 us
  transfers between devices with their start and end apart: 2, of which 1 were waited for; matrix products, arithmetic and copies ran while one was open for 1% of the time, Pallas kernels for 0%

commit v1 on v0

--- a/solution.py
+++ b/solution.py
@@ -5,6 +5,14 @@
 
 ITERS = 20
 highest = lax.Precision.HIGHEST
+
+
+def doubling_sum(x, mesh_axis):
+    peers, total = (lax.axis_size(mesh_axis), x)
+    for hop in [1 << k for k in range(peers.bit_length() - 1)]:
+        swap = [(i, i ^ hop) for i in range(peers)]
+        total = total + lax.ppermute(total, mesh_axis, swap)
+    return total
 
 
 def off_flags(moments, starts, range_len):
@@ -51,7 +59,7 @@
     pixel_ids = position * pixels + jnp.arange(pixels, dtype=jnp.int32)
     selector = (pixel_ids[:, None] == pointing[None, :]).astype(jnp.bfloat16)
     steer_local = jnp.einsum("rpx,xb->rpb", patterns, selector, preferred_element_type=jnp.float32)
-    steering = lax.psum(steer_local, "tm")
+    steering = doubling_sum(steer_local, "tm")
     blocks = voltages.reshape(devices, per_dev, samples_dev, double_width)
     arrived = lax.all_to_all(blocks, "tm", split_axis=0, concat_axis=0, tiled=True)
     moments = (

time: 553 us -> 514 us (0.929)
  blocking collectives: 81.9 us -> 0 us
  waiting for transfers between devices: 60.6 us -> 95.5 us
  starting transfers between devices: 7.43 us -> 14.3 us
    psum x1 -> x0, blocking collectives: 81.9 us -> none  [on_device(): steering = lax.psum(steer_local, 'tm')]
    ppermute x0 -> x4, waiting for transfers between devices: none -> 33.2 us  [doubling_sum(): total = total + lax.ppermute(total, mesh_axis, swap)]
    ppermute x0 -> x4, starting transfers between devices: none -> 6.85 us  [doubling_sum(): total = total + lax.ppermute(total, mesh_axis, swap)]
  transfers between devices with their start and end apart: 2 -> 6, of which waited for: 1 -> 5; matrix products, arithmetic and copies ran while one was open for 1% -> 1% of each run, Pallas kernels for 0% -> 0%
where the time goes in v1:
time: 514 us; the launch traced here: 513 us
  matrix products  303 us (59%)
  waiting for transfers between devices  95.5 us (19%)
  other arithmetic  43.7 us (9%)
  local copies, waits for them, and re-layouts  40.6 us (8%)
  starting transfers between devices  14.3 us (3%)
  between operations  14.2 us (3%)
    dot_general x80, matrix products, apply_white(): return jnp.einsum('kij,kjb->kib', matrix, vector, precision=highest)  294 us
    all_gather x1, waiting for transfers between devices, on_device(): collected = lax.all_gather(flat_pair, 'tm', axis=0, tiled=True)  62.3 us
    ppermute x4, waiting for transfers between devices, doubling_sum(): total = total + lax.ppermute(total, mesh_axis, swap)  33.2 us
    mul x20, other arithmetic, power_turn(): return (image_real * factor[:, None, :], image_imag * factor[:, None, :])  26.1 us
    unnamed x11, local copies, waits for them, and re-layouts  11.5 us
  transfers between devices with their start and end apart: 6, of which 5 were waited for; matrix products, arithmetic and copies ran while one was open for 1% of the time, Pallas kernels for 0%

profile of v1, /device:TPU:0, one launch (start us, length us, event | category | flops | bytes accessed | tf_op | source)
XLA Modules:
  0.0 513.0 jit_solution(11280824664189523284)
XLA Ops:
  7.2 7.9 %copy.28 = bf16[256,8,2,188]{3,2,1,0:T(2,128)(2,1)S(1)} copy(bf16[256,8,2,188]{0,2,3,1:T(2,128)(2,1)} %param.6) | data formatting | bytes 3080192 | tf_op args[0]
  17.1 7.4 %all-to-all-start = ((bf16[16,16,8,376]{3,2,1,0:T(8,128)(2,1)}), bf16[16,16,8,376]{3,2,1,0:T(8,128)(2,1)S(1)}, u32[]{:S(2)}, u32[]{:S(2)}) async-start(bf16[16,16,8,376]{3,2,1,0:T(8,128)(2,1)} %reshape.61), calls=%async_computation | async-start | bytes 3145728 | tf_op jit(solution)/shard_map/all_to_all | solution.py:64
  28.1 10.7 %collective-permute-done.1 = f32[2,188,36]{1,2,0:T(8,128)S(1)} collective-permute-done((f32[2,188,36]{1,2,0:T(8,128)S(1)}, f32[2,188,36]{1,2,0:T(8,128)S(1)}, u32[]{:S(2)}, u32[]{:S(2)}) %collective-permute-start.1) | collective-permute-done | bytes 54176 | tf_op jit(solution)/shard_map/ppermute | solution.py:14
  39.0 13.8 %collective-permute-done.2 = f32[2,188,36]{1,2,0:T(8,128)S(1)} collective-permute-done((f32[2,188,36]{1,2,0:T(8,128)S(1)}, f32[2,188,36]{1,2,0:T(8,128)S(1)}, u32[]{:S(2)}, u32[]{:S(2)}) %collective-permute-start.2) | collective-permute-done | bytes 54176 | tf_op jit(solution)/shard_map/ppermute | solution.py:14
  52.8 4.4 collective-permute-start.3
  57.9 7.9 %collective-permute-done.3 = f32[2,188,36]{1,2,0:T(8,128)S(1)} collective-permute-done((f32[2,188,36]{1,2,0:T(8,128)S(1)}, f32[2,188,36]{1,2,0:T(8,128)S(1)}, u32[]{:S(2)}, u32[]{:S(2)}) %collective-permute-start.3) | collective-permute-done | bytes 54176 | tf_op jit(solution)/shard_map/ppermute | solution.py:14
  74.4 321.9 %while.12 = (s32[]{:T(128)}, f32[16,188,36]{1,2,0:T(8,128)}, f32[16,188,36]{1,2,0:T(8,128)}, f32[1,188,36]{1,2,0:T(8,128)S(1)}, f32[1,188,36]{1,2,0:T(8,128)S(1)...) while((s32[]{:T(128)}, f32[16,188,36]{1,2,0:T(8,128)}, f32[16,188,36]{1,2,0:T(8,128)}, ...), condition=%wide.region_7.8_spmd, body=%wide.region_4.7_spmd.sunk | while | flops 980656704 | bytes 30075944 | solution.py:104
  74.4 5.4 %fusion.50 = f32[16,36,188]{2,1,0:T(8,128)S(1)} fusion(f32[16,188,188]{2,1,0:T(8,128)} %get-tuple-element.155, f32[16,188,36]{1,2,0:T(8,128)} %get-tuple-element.143, f32[16,188,36]{1,2,0:T(8,128)} %get-tuple-element.144, f32[188,36]{0,1:T(8,128)S(1)} %bitcast.63, f32[188,36]{0,1:T(8,128)S(1)} %bitcast.68), kind=kOutput, calls=%fused_computation.13.clone.1 | convolution fusion | flops 244622592 | bytes 3615616 | tf_op jit(solution)/shard_map/while/body/eval_jaxpr/kij,kjb->kib/dot_general | solution.py:84
  90.5 5.4 %fusion.50 = f32[16,36,188]{2,1,0:T(8,128)S(1)} fusion(f32[16,188,188]{2,1,0:T(8,128)} %get-tuple-element.155, f32[16,188,36]{1,2,0:T(8,128)} %get-tuple-element.143, f32[16,188,36]{1,2,0:T(8,128)} %get-tuple-element.144, f32[188,36]{0,1:T(8,128)S(1)} %bitcast.63, f32[188,36]{0,1:T(8,128)S(1)} %bitcast.68), kind=kOutput, calls=%fused_computation.13.clone.1 | convolution fusion | flops 244622592 | bytes 3615616 | tf_op jit(solution)/shard_map/while/body/eval_jaxpr/kij,kjb->kib/dot_general | solution.py:84
  106.6 5.4 %fusion.50 = f32[16,36,188]{2,1,0:T(8,128)S(1)} fusion(f32[16,188,188]{2,1,0:T(8,128)} %get-tuple-element.155, f32[16,188,36]{1,2,0:T(8,128)} %get-tuple-element.143, f32[16,188,36]{1,2,0:T(8,128)} %get-tuple-element.144, f32[188,36]{0,1:T(8,128)S(1)} %bitcast.63, f32[188,36]{0,1:T(8,128)S(1)} %bitcast.68), kind=kOutput, calls=%fused_computation.13.clone.1 | convolution fusion | flops 244622592 | bytes 3615616 | tf_op jit(solution)/shard_map/while/body/eval_jaxpr/kij,kjb->kib/dot_general | solution.py:84
  122.7 5.4 %fusion.50 = f32[16,36,188]{2,1,0:T(8,128)S(1)} fusion(f32[16,188,188]{2,1,0:T(8,128)} %get-tuple-element.155, f32[16,188,36]{1,2,0:T(8,128)} %get-tuple-element.143, f32[16,188,36]{1,2,0:T(8,128)} %get-tuple-element.144, f32[188,36]{0,1:T(8,128)S(1)} %bitcast.63, f32[188,36]{0,1:T(8,128)S(1)} %bitcast.68), kind=kOutput, calls=%fused_computation.13.clone.1 | convolution fusion | flops 244622592 | bytes 3615616 | tf_op jit(solution)/shard_map/while/body/eval_jaxpr/kij,kjb->kib/dot_general | solution.py:84
  138.8 5.4 %fusion.50 = f32[16,36,188]{2,1,0:T(8,128)S(1)} fusion(f32[16,188,188]{2,1,0:T(8,128)} %get-tuple-element.155, f32[16,188,36]{1,2,0:T(8,128)} %get-tuple-element.143, f32[16,188,36]{1,2,0:T(8,128)} %get-tuple-element.144, f32[188,36]{0,1:T(8,128)S(1)} %bitcast.63, f32[188,36]{0,1:T(8,128)S(1)} %bitcast.68), kind=kOutput, calls=%fused_computation.13.clone.1 | convolution fusion | flops 244622592 | bytes 3615616 | tf_op jit(solution)/shard_map/while/body/eval_jaxpr/kij,kjb->kib/dot_general | solution.py:84
  154.9 5.4 %fusion.50 = f32[16,36,188]{2,1,0:T(8,128)S(1)} fusion(f32[16,188,188]{2,1,0:T(8,128)} %get-tuple-element.155, f32[16,188,36]{1,2,0:T(8,128)} %get-tuple-element.143, f32[16,188,36]{1,2,0:T(8,128)} %get-tuple-element.144, f32[188,36]{0,1:T(8,128)S(1)} %bitcast.63, f32[188,36]{0,1:T(8,128)S(1)} %bitcast.68), kind=kOutput, calls=%fused_computation.13.clone.1 | convolution fusion | flops 244622592 | bytes 3615616 | tf_op jit(solution)/shard_map/while/body/eval_jaxpr/kij,kjb->kib/dot_general | solution.py:84
  171.0 5.4 %fusion.50 = f32[16,36,188]{2,1,0:T(8,128)S(1)} fusion(f32[16,188,188]{2,1,0:T(8,128)} %get-tuple-element.155, f32[16,188,36]{1,2,0:T(8,128)} %get-tuple-element.143, f32[16,188,36]{1,2,0:T(8,128)} %get-tuple-element.144, f32[188,36]{0,1:T(8,128)S(1)} %bitcast.63, f32[188,36]{0,1:T(8,128)S(1)} %bitcast.68), kind=kOutput, calls=%fused_computation.13.clone.1 | convolution fusion | flops 244622592 | bytes 3615616 | tf_op jit(solution)/shard_map/while/body/eval_jaxpr/kij,kjb->kib/dot_general | solution.py:84
  187.1 5.4 %fusion.50 = f32[16,36,188]{2,1,0:T(8,128)S(1)} fusion(f32[16,188,188]{2,1,0:T(8,128)} %get-tuple-element.155, f32[16,188,36]{1,2,0:T(8,128)} %get-tuple-element.143, f32[16,188,36]{1,2,0:T(8,128)} %get-tuple-element.144, f32[188,36]{0,1:T(8,128)S(1)} %bitcast.63, f32[188,36]{0,1:T(8,128)S(1)} %bitcast.68), kind=kOutput, calls=%fused_computation.13.clone.1 | convolution fusion | flops 244622592 | bytes 3615616 | tf_op jit(solution)/shard_map/while/body/eval_jaxpr/kij,kjb->kib/dot_general | solution.py:84
  203.2 5.4 %fusion.50 = f32[16,36,188]{2,1,0:T(8,128)S(1)} fusion(f32[16,188,188]{2,1,0:T(8,128)} %get-tuple-element.155, f32[16,188,36]{1,2,0:T(8,128)} %get-tuple-element.143, f32[16,188,36]{1,2,0:T(8,128)} %get-tuple-element.144, f32[188,36]{0,1:T(8,128)S(1)} %bitcast.63, f32[188,36]{0,1:T(8,128)S(1)} %bitcast.68), kind=kOutput, calls=%fused_computation.13.clone.1 | convolution fusion | flops 244622592 | bytes 3615616 | tf_op jit(solution)/shard_map/while/body/eval_jaxpr/kij,kjb->kib/dot_general | solution.py:84
  219.3 5.4 %fusion.50 = f32[16,36,188]{2,1,0:T(8,128)S(1)} fusion(f32[16,188,188]{2,1,0:T(8,128)} %get-tuple-element.155, f32[16,188,36]{1,2,0:T(8,128)} %get-tuple-element.143, f32[16,188,36]{1,2,0:T(8,128)} %get-tuple-element.144, f32[188,36]{0,1:T(8,128)S(1)} %bitcast.63, f32[188,36]{0,1:T(8,128)S(1)} %bitcast.68), kind=kOutput, calls=%fused_computation.13.clone.1 | convolution fusion | flops 244622592 | bytes 3615616 | tf_op jit(solution)/shard_map/while/body/eval_jaxpr/kij,kjb->kib/dot_general | solution.py:84
  235.3 5.4 %fusion.50 = f32[16,36,188]{2,1,0:T(8,128)S(1)} fusion(f32[16,188,188]{2,1,0:T(8,128)} %get-tuple-element.155, f32[16,188,36]{1,2,0:T(8,128)} %get-tuple-element.143, f32[16,188,36]{1,2,0:T(8,128)} %get-tuple-element.144, f32[188,36]{0,1:T(8,128)S(1)} %bitcast.63, f32[188,36]{0,1:T(8,128)S(1)} %bitcast.68), kind=kOutput, calls=%fused_computation.13.clone.1 | convolution fusion | flops 244622592 | bytes 3615616 | tf_op jit(solution)/shard_map/while/body/eval_jaxpr/kij,kjb->kib/dot_general | solution.py:84
  251.4 5.4 %fusion.50 = f32[16,36,188]{2,1,0:T(8,128)S(1)} fusion(f32[16,188,188]{2,1,0:T(8,128)} %get-tuple-element.155, f32[16,188,36]{1,2,0:T(8,128)} %get-tuple-element.143, f32[16,188,36]{1,2,0:T(8,128)} %get-tuple-element.144, f32[188,36]{0,1:T(8,128)S(1)} %bitcast.63, f32[188,36]{0,1:T(8,128)S(1)} %bitcast.68), kind=kOutput, calls=%fused_computation.13.clone.1 | convolution fusion | flops 244622592 | bytes 3615616 | tf_op jit(solution)/shard_map/while/body/eval_jaxpr/kij,kjb->kib/dot_general | solution.py:84
  267.5 5.4 %fusion.50 = f32[16,36,188]{2,1,0:T(8,128)S(1)} fusion(f32[16,188,188]{2,1,0:T(8,128)} %get-tuple-element.155, f32[16,188,36]{1,2,0:T(8,128)} %get-tuple-element.143, f32[16,188,36]{1,2,0:T(8,128)} %get-tuple-element.144, f32[188,36]{0,1:T(8,128)S(1)} %bitcast.63, f32[188,36]{0,1:T(8,128)S(1)} %bitcast.68), kind=kOutput, calls=%fused_computation.13.clone.1 | convolution fusion | flops 244622592 | bytes 3615616 | tf_op jit(solution)/shard_map/while/body/eval_jaxpr/kij,kjb->kib/dot_general | solution.py:84
  283.6 5.4 %fusion.50 = f32[16,36,188]{2,1,0:T(8,128)S(1)} fusion(f32[16,188,188]{2,1,0:T(8,128)} %get-tuple-element.155, f32[16,188,36]{1,2,0:T(8,128)} %get-tuple-element.143, f32[16,188,36]{1,2,0:T(8,128)} %get-tuple-element.144, f32[188,36]{0,1:T(8,128)S(1)} %bitcast.63, f32[188,36]{0,1:T(8,128)S(1)} %bitcast.68), kind=kOutput, calls=%fused_computation.13.clone.1 | convolution fusion | flops 244622592 | bytes 3615616 | tf_op jit(solution)/shard_map/while/body/eval_jaxpr/kij,kjb->kib/dot_general | solution.py:84
  299.7 5.4 %fusion.50 = f32[16,36,188]{2,1,0:T(8,128)S(1)} fusion(f32[16,188,188]{2,1,0:T(8,128)} %get-tuple-element.155, f32[16,188,36]{1,2,0:T(8,128)} %get-tuple-element.143, f32[16,188,36]{1,2,0:T(8,128)} %get-tuple-element.144, f32[188,36]{0,1:T(8,128)S(1)} %bitcast.63, f32[188,36]{0,1:T(8,128)S(1)} %bitcast.68), kind=kOutput, calls=%fused_computation.13.clone.1 | convolution fusion | flops 244622592 | bytes 3615616 | tf_op jit(solution)/shard_map/while/body/eval_jaxpr/kij,kjb->kib/dot_general | solution.py:84
  315.8 5.4 %fusion.50 = f32[16,36,188]{2,1,0:T(8,128)S(1)} fusion(f32[16,188,188]{2,1,0:T(8,128)} %get-tuple-element.155, f32[16,188,36]{1,2,0:T(8,128)} %get-tuple-element.143, f32[16,188,36]{1,2,0:T(8,128)} %get-tuple-element.144, f32[188,36]{0,1:T(8,128)S(1)} %bitcast.63, f32[188,36]{0,1:T(8,128)S(1)} %bitcast.68), kind=kOutput, calls=%fused_computation.13.clone.1 | convolution fusion | flops 244622592 | bytes 3615616 | tf_op jit(solution)/shard_map/while/body/eval_jaxpr/kij,kjb->kib/dot_general | solution.py:84
  331.9 5.4 %fusion.50 = f32[16,36,188]{2,1,0:T(8,128)S(1)} fusion(f32[16,188,188]{2,1,0:T(8,128)} %get-tuple-element.155, f32[16,188,36]{1,2,0:T(8,128)} %get-tuple-element.143, f32[16,188,36]{1,2,0:T(8,128)} %get-tuple-element.144, f32[188,36]{0,1:T(8,128)S(1)} %bitcast.63, f32[188,36]{0,1:T(8,128)S(1)} %bitcast.68), kind=kOutput, calls=%fused_computation.13.clone.1 | convolution fusion | flops 244622592 | bytes 3615616 | tf_op jit(solution)/shard_map/while/body/eval_jaxpr/kij,kjb->kib/dot_general | solution.py:84
  348.0 5.4 %fusion.50 = f32[16,36,188]{2,1,0:T(8,128)S(1)} fusion(f32[16,188,188]{2,1,0:T(8,128)} %get-tuple-element.155, f32[16,188,36]{1,2,0:T(8,128)} %get-tuple-element.143, f32[16,188,36]{1,2,0:T(8,128)} %get-tuple-element.144, f32[188,36]{0,1:T(8,128)S(1)} %bitcast.63, f32[188,36]{0,1:T(8,128)S(1)} %bitcast.68), kind=kOutput, calls=%fused_computation.13.clone.1 | convolution fusion | flops 244622592 | bytes 3615616 | tf_op jit(solution)/shard_map/while/body/eval_jaxpr/kij,kjb->kib/dot_general | solution.py:84
  364.1 5.4 %fusion.50 = f32[16,36,188]{2,1,0:T(8,128)S(1)} fusion(f32[16,188,188]{2,1,0:T(8,128)} %get-tuple-element.155, f32[16,188,36]{1,2,0:T(8,128)} %get-tuple-element.143, f32[16,188,36]{1,2,0:T(8,128)} %get-tuple-element.144, f32[188,36]{0,1:T(8,128)S(1)} %bitcast.63, f32[188,36]{0,1:T(8,128)S(1)} %bitcast.68), kind=kOutput, calls=%fused_computation.13.clone.1 | convolution fusion | flops 244622592 | bytes 3615616 | tf_op jit(solution)/shard_map/while/body/eval_jaxpr/kij,kjb->kib/dot_general | solution.py:84
  380.2 5.4 %fusion.50 = f32[16,36,188]{2,1,0:T(8,128)S(1)} fusion(f32[16,188,188]{2,1,0:T(8,128)} %get-tuple-element.155, f32[16,188,36]{1,2,0:T(8,128)} %get-tuple-element.143, f32[16,188,36]{1,2,0:T(8,128)} %get-tuple-element.144, f32[188,36]{0,1:T(8,128)S(1)} %bitcast.63, f32[188,36]{0,1:T(8,128)S(1)} %bitcast.68), kind=kOutput, calls=%fused_computation.13.clone.1 | convolution fusion | flops 244622592 | bytes 3615616 | tf_op jit(solution)/shard_map/while/body/eval_jaxpr/kij,kjb->kib/dot_general | solution.py:84
  401.3 62.3 %all-gather.2.cloned.1.call-done = bf16[256,2,6768]{2,0,1:T(8,128)(2,1)} async-done(((bf16[16,2,6768]{2,0,1:T(8,128)(2,1)}), bf16[256,2,6768]{2,0,1:T(8,128)(2,1)}) %all-gather.2.cloned.1.call-update) | async-done | bytes 6930448 | tf_op jit(solution)/shard_map/all_gather | solution.py:111
  463.6 10.1 %copy.29 = bf16[256,2,6768]{0,2,1:T(8,128)(2,1)} copy(bf16[256,2,6768]{2,0,1:T(8,128)(2,1)} %all-gather.2.cloned.1.call-done) | data formatting | bytes 13860864 | tf_op jit(solution)/shard_map/all_gather | solution.py:111
  473.7 9.9 %reshape.63 = bf16[256,2,36,188]{0,3,2,1:T(8,128)(2,1)} reshape(bf16[256,2,6768]{0,2,1:T(8,128)(2,1)} %copy.29) | data formatting | bytes 13860864 | tf_op jit(solution)/shard_map/reshape | solution.py:112
  488.9 7.0 %maximum_bitcast_fusion = (bf16[256,36,1,376]{0,3,2,1:T(8,128)(2,1)}, bf16[256,36,1,376]{0,3,2,1:T(8,128)(2,1)}) fusion(bf16[256,36,188]{0,2,1:T(8,128)(2,1)S(1)} %get-tuple-element.71, bf16[256,36,188]{0,2,1:T(8,128)(2,1)S(1)} %get-tuple-element.72, bf16[256,36,188]{0,2,1:T(8,128)(2,1)S(1)} %fusion.32), kind=kLoop, calls=%fused_computation.19 | loop fusion | flops 27721728 | bytes 24256512 | tf_op jit(solution)/shard_map/stack | solution.py:37
  496.0 7.2 %fusion.4 = f32[256,36,2,128]{3,0,2,1:T(8,128)S(1)} fusion(bf16[256,36,1,376]{0,3,2,1:T(8,128)(2,1)} %get-tuple-element.74, bf16[256,36,1,376]{0,3,2,1:T(8,128)(2,1)} %get-tuple-element.73, bf16[376,128,1,1]{1,0,2,3:T(8,128)(2,1)S(1)} %reshape.67), kind=kOutput, calls=%fused_computation.15 | convolution fusion | flops 1781121024 | bytes 23394304 | tf_op jit(solution)/shard_map/dot_general | solution.py:38
  (265 shorter events, 240.6 us)
Async XLA Ops:
  15.1 9.5 %copy-start.4 = (bf16[2,188,128]{2,0,1:T(2,128)(2,1)S(1)}, bf16[2,188,128]{2,0,1:T(2,128)(2,1)}, u32[]{:S(2)}) copy-start(bf16[2,188,128]{2,0,1:T(2,128)(2,1)} %param.9) | copy-start | bytes 288772
  15.1 9.5 %copy-start.5 = (s32[36]{0:T(128)S(1)}, s32[36]{0:T(128)}, u32[]{:S(2)}) copy-start(s32[36]{0:T(128)} %param.8) | copy-start | bytes 436
  15.1 12.9 %copy-start.6 = (s32[8]{0:T(128)S(1)}, s32[8]{0:T(128)}, u32[]{:S(2)}) copy-start(s32[8]{0:T(128)} %param.7) | copy-start | bytes 100
  17.1 48.7 %all-to-all-start = ((bf16[16,16,8,376]{3,2,1,0:T(8,128)(2,1)}), bf16[16,16,8,376]{3,2,1,0:T(8,128)(2,1)S(1)}, u32[]{:S(2)}, u32[]{:S(2)}) async-start(bf16[16,16,8,376]{3,2,1,0:T(8,128)(2,1)} %reshape.61), calls=%async_computation | async-start | bytes 3145728 | tf_op jit(solution)/shard_map/all_to_all | solution.py:64
  24.5 439.1 %all-gather.2.cloned.1.call-start = ((), (), s32[]{:S(2)}) async-start(), calls=%async_computation.1 | async-start | bytes 7380992 | tf_op jit(solution)/shard_map/all_gather | solution.py:111
  24.8 1.3 collective-permute-start
  26.1 12.7 %collective-permute-start.1 = (f32[2,188,36]{1,2,0:T(8,128)S(1)}, f32[2,188,36]{1,2,0:T(8,128)S(1)}, u32[]{:S(2)}, u32[]{:S(2)}) collective-permute-start(f32[2,188,36]{1,2,0:T(8,128)S(1)} %add.104), channel_id=1, source_target_pairs={{0,2},{1,3},{2,0},{3,1},{4,6},{5,7},{6,4},{7,5},{8,10},{9,11},{10,... | collective-permute-start | bytes 162440 | tf_op jit(solution)/shard_map/ppermute | solution.py:14
  38.8 13.9 %collective-permute-start.2 = (f32[2,188,36]{1,2,0:T(8,128)S(1)}, f32[2,188,36]{1,2,0:T(8,128)S(1)}, u32[]{:S(2)}, u32[]{:S(2)}) collective-permute-start(f32[2,188,36]{1,2,0:T(8,128)S(1)} %add.105), channel_id=1, source_target_pairs={{0,4},{1,5},{2,6},{3,7},{4,0},{5,1},{6,2},{7,3},{8,12},{9,13},{10,... | collective-permute-start | bytes 162440 | tf_op jit(solution)/shard_map/ppermute | solution.py:14
  52.8 13.0 %collective-permute-start.3 = (f32[2,188,36]{1,2,0:T(8,128)S(1)}, f32[2,188,36]{1,2,0:T(8,128)S(1)}, u32[]{:S(2)}, u32[]{:S(2)}) collective-permute-start(f32[2,188,36]{1,2,0:T(8,128)S(1)} %add.106), channel_id=1, source_target_pairs={{0,8},{1,9},{2,10},{3,11},{4,12},{5,13},{6,14},{7,15},{8,0},{9,1},... | collective-permute-start | bytes 162440 | tf_op jit(solution)/shard_map/ppermute | solution.py:14
  74.4 5.4 %copy-start.2 = (f32[16,188,36]{1,2,0:T(8,128)S(1)}, f32[16,188,36]{1,2,0:T(8,128)}, u32[]{:S(2)}) copy-start(f32[16,188,36]{1,2,0:T(8,128)} %get-tuple-element.144) | copy-start | bytes 1299460 | tf_op jit(solution)/shard_map/while
  90.5 5.4 %copy-start.2 = (f32[16,188,36]{1,2,0:T(8,128)S(1)}, f32[16,188,36]{1,2,0:T(8,128)}, u32[]{:S(2)}) copy-start(f32[16,188,36]{1,2,0:T(8,128)} %get-tuple-element.144) | copy-start | bytes 1299460 | tf_op jit(solution)/shard_map/while
  106.6 5.4 %copy-start.2 = (f32[16,188,36]{1,2,0:T(8,128)S(1)}, f32[16,188,36]{1,2,0:T(8,128)}, u32[]{:S(2)}) copy-start(f32[16,188,36]{1,2,0:T(8,128)} %get-tuple-element.144) | copy-start | bytes 1299460 | tf_op jit(solution)/shard_map/while
  122.7 5.4 %copy-start.2 = (f32[16,188,36]{1,2,0:T(8,128)S(1)}, f32[16,188,36]{1,2,0:T(8,128)}, u32[]{:S(2)}) copy-start(f32[16,188,36]{1,2,0:T(8,128)} %get-tuple-element.144) | copy-start | bytes 1299460 | tf_op jit(solution)/shard_map/while
  138.8 5.4 %copy-start.1 = (f32[16,188,36]{1,2,0:T(8,128)S(1)}, f32[16,188,36]{1,2,0:T(8,128)}, u32[]{:S(2)}) copy-start(f32[16,188,36]{1,2,0:T(8,128)} %get-tuple-element.143) | copy-start | bytes 1299460 | tf_op jit(solution)/shard_map/while
  138.8 5.4 %copy-start.2 = (f32[16,188,36]{1,2,0:T(8,128)S(1)}, f32[16,188,36]{1,2,0:T(8,128)}, u32[]{:S(2)}) copy-start(f32[16,188,36]{1,2,0:T(8,128)} %get-tuple-element.144) | copy-start | bytes 1299460 | tf_op jit(solution)/shard_map/while
  154.9 5.4 %copy-start.2 = (f32[16,188,36]{1,2,0:T(8,128)S(1)}, f32[16,188,36]{1,2,0:T(8,128)}, u32[]{:S(2)}) copy-start(f32[16,188,36]{1,2,0:T(8,128)} %get-tuple-element.144) | copy-start | bytes 1299460 | tf_op jit(solution)/shard_map/while
  171.0 5.4 %copy-start.1 = (f32[16,188,36]{1,2,0:T(8,128)S(1)}, f32[16,188,36]{1,2,0:T(8,128)}, u32[]{:S(2)}) copy-start(f32[16,188,36]{1,2,0:T(8,128)} %get-tuple-element.143) | copy-start | bytes 1299460 | tf_op jit(solution)/shard_map/while
  171.0 5.4 %copy-start.2 = (f32[16,188,36]{1,2,0:T(8,128)S(1)}, f32[16,188,36]{1,2,0:T(8,128)}, u32[]{:S(2)}) copy-start(f32[16,188,36]{1,2,0:T(8,128)} %get-tuple-element.144) | copy-start | bytes 1299460 | tf_op jit(solution)/shard_map/while
  187.1 5.4 %copy-start.2 = (f32[16,188,36]{1,2,0:T(8,128)S(1)}, f32[16,188,36]{1,2,0:T(8,128)}, u32[]{:S(2)}) copy-start(f32[16,188,36]{1,2,0:T(8,128)} %get-tuple-element.144) | copy-start | bytes 1299460 | tf_op jit(solution)/shard_map/while
  203.2 5.4 %copy-start.1 = (f32[16,188,36]{1,2,0:T(8,128)S(1)}, f32[16,188,36]{1,2,0:T(8,128)}, u32[]{:S(2)}) copy-start(f32[16,188,36]{1,2,0:T(8,128)} %get-tuple-element.143) | copy-start | bytes 1299460 | tf_op jit(solution)/shard_map/while
  203.2 5.4 %copy-start.2 = (f32[16,188,36]{1,2,0:T(8,128)S(1)}, f32[16,188,36]{1,2,0:T(8,128)}, u32[]{:S(2)}) copy-start(f32[16,188,36]{1,2,0:T(8,128)} %get-tuple-element.144) | copy-start | bytes 1299460 | tf_op jit(solution)/shard_map/while
  219.3 5.4 %copy-start.2 = (f32[16,188,36]{1,2,0:T(8,128)S(1)}, f32[16,188,36]{1,2,0:T(8,128)}, u32[]{:S(2)}) copy-start(f32[16,188,36]{1,2,0:T(8,128)} %get-tuple-element.144) | copy-start | bytes 1299460 | tf_op jit(solution)/shard_map/while
  235.3 5.4 %copy-start.2 = (f32[16,188,36]{1,2,0:T(8,128)S(1)}, f32[16,188,36]{1,2,0:T(8,128)}, u32[]{:S(2)}) copy-start(f32[16,188,36]{1,2,0:T(8,128)} %get-tuple-element.144) | copy-start | bytes 1299460 | tf_op jit(solution)/shard_map/while
  251.4 5.4 %copy-start.2 = (f32[16,188,36]{1,2,0:T(8,128)S(1)}, f32[16,188,36]{1,2,0:T(8,128)}, u32[]{:S(2)}) copy-start(f32[16,188,36]{1,2,0:T(8,128)} %get-tuple-element.144) | copy-start | bytes 1299460 | tf_op jit(solution)/shard_map/while
  267.5 5.4 %copy-start.2 = (f32[16,188,36]{1,2,0:T(8,128)S(1)}, f32[16,188,36]{1,2,0:T(8,128)}, u32[]{:S(2)}) copy-start(f32[16,188,36]{1,2,0:T(8,128)} %get-tuple-element.144) | copy-start | bytes 1299460 | tf_op jit(solution)/shard_map/while
  283.6 5.4 %copy-start.2 = (f32[16,188,36]{1,2,0:T(8,128)S(1)}, f32[16,188,36]{1,2,0:T(8,128)}, u32[]{:S(2)}) copy-start(f32[16,188,36]{1,2,0:T(8,128)} %get-tuple-element.144) | copy-start | bytes 1299460 | tf_op jit(solution)/shard_map/while
  299.7 5.4 %copy-start.2 = (f32[16,188,36]{1,2,0:T(8,128)S(1)}, f32[16,188,36]{1,2,0:T(8,128)}, u32[]{:S(2)}) copy-start(f32[16,188,36]{1,2,0:T(8,128)} %get-tuple-element.144) | copy-start | bytes 1299460 | tf_op jit(solution)/shard_map/while
  315.8 5.4 %copy-start.2 = (f32[16,188,36]{1,2,0:T(8,128)S(1)}, f32[16,188,36]{1,2,0:T(8,128)}, u32[]{:S(2)}) copy-start(f32[16,188,36]{1,2,0:T(8,128)} %get-tuple-element.144) | copy-start | bytes 1299460 | tf_op jit(solution)/shard_map/while
  331.9 5.4 %copy-start.2 = (f32[16,188,36]{1,2,0:T(8,128)S(1)}, f32[16,188,36]{1,2,0:T(8,128)}, u32[]{:S(2)}) copy-start(f32[16,188,36]{1,2,0:T(8,128)} %get-tuple-element.144) | copy-start | bytes 1299460 | tf_op jit(solution)/shard_map/while
  348.0 5.4 %copy-start.2 = (f32[16,188,36]{1,2,0:T(8,128)S(1)}, f32[16,188,36]{1,2,0:T(8,128)}, u32[]{:S(2)}) copy-start(f32[16,188,36]{1,2,0:T(8,128)} %get-tuple-element.144) | copy-start | bytes 1299460 | tf_op jit(solution)/shard_map/while
  364.1 5.4 %copy-start.2 = (f32[16,188,36]{1,2,0:T(8,128)S(1)}, f32[16,188,36]{1,2,0:T(8,128)}, u32[]{:S(2)}) copy-start(f32[16,188,36]{1,2,0:T(8,128)} %get-tuple-element.144) | copy-start | bytes 1299460 | tf_op jit(solution)/shard_map/while
  380.2 5.4 %copy-start.2 = (f32[16,188,36]{1,2,0:T(8,128)S(1)}, f32[16,188,36]{1,2,0:T(8,128)}, u32[]{:S(2)}) copy-start(f32[16,188,36]{1,2,0:T(8,128)} %get-tuple-element.144) | copy-start | bytes 1299460 | tf_op jit(solution)/shard_map/while
  (38 other events, 159.4 us)
Sparse Core Ops, SparseCore 0:
  399.3 64.2 all-gather.1
